TPU v7x, 128 devices: a whole 4x4x4 slice. The times are simulated.
128 devices in a mesh: orig: 8 (over x, core), dest: 16 (over y, z).
Axes of the slice: x: 4, y: 4, z: 4, core: 2. Of those that a mesh axis runs over, the one named last changes fastest.
Arguments:
- root_blocks: bfloat16 [1024, 1024, 1024], P(('orig', 'dest')), may hold values from 0.0099487305 to 1
- sector_map: int32 [1024], replicated, may hold values from 0 to 127
- dest_owner: int32 [1024, 1], P(('orig', 'dest')), may hold values from 0 to 15; in each aligned block of 8 rows (0 to 7, 8 to 15, ...) at most 2 rows name the same one
- local_row: int32 [1024], P(('orig', 'dest')), may hold values from 0 to 7
- local_col: int32 [1024], P(('orig', 'dest')), may hold values from 0 to 3
- present: int32 [1024], P(('orig', 'dest')), may hold values 0 or 1
- prior: float32 [8192, 8192], P('orig', 'dest'), may hold values from 1 to 30
- row_target: float32 [8192], P('orig'), may hold values from 4096 to 16384
- col_target: float32 [8192], P('dest'), may hold values from 4096 to 16384
Outputs:
- balanced: float32 [8192, 8192], P('orig', 'dest')
Inputs may be any that keep to these rules, and one draw needn't show every extreme that they name: Among the 8 root blocks of one device, no value of dest_owner occurs more than 2 times; some device has one that occurs exactly 2 times.
All inputs are finite; a program needn't handle non-finite values. No bound on the sum of `present` on one device may be relied on, other than what follows from the above.
Results may differ from a plain program's by a relative error of at most 0.0003.
Values sent between devices are 32-bit elements; how exact they have to be, the bound alone decides.
A program may use at most 128 MiB of HBM per device.

v0:
```python
import jax
import jax.numpy as jnp
from jax import lax
from jax.sharding import PartitionSpec as P

S_T = 128


def shards(
    root_blocks,
    sector_map,
    dest_owner,
    local_row,
    local_col,
    present,
    prior,
    row_target,
    col_target,
):
    n_dest = lax.axis_size("dest")
    rows_here = prior.shape[0]
    cols_here = prior.shape[1]
    s_t = S_T
    tro = rows_here // s_t
    trd = cols_here // s_t
    highest = lax.Precision.HIGHEST
    concord = (sector_map[:, None] == jnp.arange(s_t, dtype=jnp.int32)[None, :]).astype(
        jnp.bfloat16
    )
    concord_wide = concord.astype(jnp.float32)
    left = jnp.einsum("sk,bsj->bkj", concord, root_blocks, preferred_element_type=jnp.float32)
    aggregated = jnp.einsum(
        "bkj,jl->bkl", left, concord_wide, preferred_element_type=jnp.float32, precision=highest
    )
    aggregated = aggregated * present.astype(jnp.float32)[:, None, None]
    owner = dest_owner[:, 0]
    target_local = local_row * trd + local_col
    global_slot = owner * (tro * trd) + target_local
    picker = (
        jnp.arange(n_dest * tro * trd, dtype=jnp.int32)[:, None] == global_slot[None, :]
    ).astype(jnp.float32)
    dense = jnp.einsum(
        "pb,bkl->pkl", picker, aggregated, preferred_element_type=jnp.float32, precision=highest
    )
    received = lax.psum_scatter(dense, "dest", scatter_dimension=0, tiled=True)
    added = received.reshape(tro, trd, s_t, s_t).transpose(0, 2, 1, 3).reshape(rows_here, cols_here)
    table = prior + added
    row_sums = lax.psum(jnp.sum(table, axis=1), "dest")
    row_factor = row_target / row_sums
    scaled = table * row_factor[:, None]
    col_sums = lax.psum(jnp.sum(scaled, axis=0), "orig")
    col_factor = col_target / col_sums
    return scaled * col_factor[None, :]


def solution(mesh):
    placed = (
        P(("orig", "dest"), None, None),
        P(),
        P(("orig", "dest"), None),
        P(("orig", "dest")),
        P(("orig", "dest")),
        P(("orig", "dest")),
        P("orig", "dest"),
        P("orig"),
        P("dest"),
    )
    return jax.shard_map(
        shards, mesh=mesh, in_specs=placed, out_specs=P("orig", "dest"), check_vma=False
    )
```

profile of v0, /device:TPU:1, one launch (start us, length us, event | category | flops | bytes accessed | tf_op | source)
XLA Modules:
  0.0 301.5 jit_solution(12025145763176269876)
XLA Ops:
  6.5 0.0 reduce-scatter.2.cloned.1.call-start
  6.5 0.7 convert_element_type.2
  7.2 0.0 copy-start.1
  7.2 8.7 %fusion.8 = f32[128,8,1024]{2,0,1:T(8,128)S(1)} fusion(bf16[8,1024,1024]{2,1,0:T(8,128)(2,1)} %param.9, s32[1024]{0:T(1024)} %param.10), kind=kOutput, calls=%fused_computation.9 | convolution fusion | flops 2147614720 | bytes 20975616 | tf_op jit(solution)/shard_map/sk,bsj->bkj/dot_general | solution.py:31
  15.9 0.0 copy-done.1
  15.9 0.0 copy-start.4
  15.9 0.0 copy-start.5
  15.9 0.0 copy-start.6
  16.0 4.3 %fusion.3 = f32[8,128,128]{2,0,1:T(8,128)S(1)} fusion(f32[128,8,1024]{2,0,1:T(8,128)S(1)} %fusion.8, f32[8]{0:T(128)S(1)} %convert_element_type.2, s32[1024]{0:T(1024)S(1)} %copy-done.1), kind=kOutput, calls=%fused_computation.6 | convolution fusion | flops 1610874880 | bytes 4722720 | tf_op jit(solution)/shard_map/bkj,jl->bkl/dot_general | solution.py:32
  20.2 0.0 copy-done.4
  20.3 0.0 copy-done.5
  20.3 0.0 copy-done.6
  20.3 17.4 %fusion.13 = f32[512,128,128]{2,0,1:T(8,128)} fusion(f32[8,128,128]{2,0,1:T(8,128)S(1)} %fusion.3, s32[8]{0:T(128)S(1)} %bitcast_add_fusion.1), kind=kOutput, calls=%fused_computation.14 | convolution fusion | flops 805310464 | bytes 34078752 | tf_op jit(solution)/shard_map/pb,bkl->pkl/dot_general | solution.py:42
  37.7 0.0 reduce-scatter.2.cloned.1.call-update
  37.7 198.4 %reduce-scatter.2.cloned.1.call-done = f32[32,128,128]{2,0,1:T(8,128)} async-done(((f32[512,128,128]{2,0,1:T(8,128)}), f32[32,128,128]{2,0,1:T(8,128)}) %reduce-scatter.2.cloned.1.call-update) | async-done | bytes 2097168 | tf_op jit(solution)/shard_map/reduce_scatter | solution.py:45
  236.1 0.0 copy-start
  236.1 2.1 copy.10
  238.2 0.1 copy-done
  238.3 0.0 copy-start.2
  238.3 0.3 fusion.16
  238.6 31.1 %psum.14 = f32[1024]{0:T(1024)S(1)} all-reduce(f32[1024]{0:T(1024)S(1)} %fusion.16), channel_id=1, replica_groups=mesh['orig'=8,'dest'=16] {'dest'}, use_global_device_ids=true, to_apply=%region_2.0 | all-reduce | flops 1024 | bytes 8192 | tf_op jit(solution)/shard_map/psum | solution.py:48
  269.7 0.0 copy-done.2
  269.7 0.0 copy-start.3
  269.7 1.9 multiply_reduce_fusion
  271.6 19.9 %psum.15 = f32[512]{0:T(512)S(1)} all-reduce(f32[512]{0:T(512)S(1)} %multiply_reduce_fusion), channel_id=1, replica_groups=mesh['orig'=8,'dest'=16] {'orig'}, use_global_device_ids=true, to_apply=%region_4.0 | all-reduce | flops 512 | bytes 4096 | tf_op jit(solution)/shard_map/psum | solution.py:51
  291.4 0.0 copy-done.3
  291.4 3.2 %multiply_multiply_fusion = f32[1024,512]{1,0:T(8,128)} fusion(f32[512]{0:T(512)S(1)} %div.7, f32[1024]{0:T(1024)S(1)} %div.6, f32[1024,512]{1,0:T(8,128)} %param.15, f32[128,8,4,128]{3,2,1,0:T(4,128)S(1)} %bitcast.31), kind=kLoop, calls=%fused_computation.4 | loop fusion | flops 1572864 | bytes 6297600 | tf_op jit(solution)/shard_map/mul | solution.py:53
  (3 shorter events, 0.0 us)
Async XLA Ops:
  6.5 229.6 %reduce-scatter.2.cloned.1.call-start = ((), (), s32[]{:S(2)}) async-start(), calls=%async_computation.1 | async-start | bytes 35651584 | tf_op jit(solution)/shard_map/reduce_scatter | solution.py:45
  7.2 8.7 %copy-start.1 = (s32[1024]{0:T(1024)S(1)}, s32[1024]{0:T(1024)}, u32[]{:S(2)}) copy-start(s32[1024]{0:T(1024)} %param.10) | copy-start | bytes 12292
  15.9 4.3 %copy-start.4 = (s32[8]{0:T(128)S(1)}, s32[8]{0:T(128)}, u32[]{:S(2)}) copy-start(s32[8]{0:T(128)} %param.13) | copy-start | bytes 100
  15.9 4.3 %copy-start.5 = (s32[8]{0:T(128)S(1)}, s32[8]{0:T(128)}, u32[]{:S(2)}) copy-start(s32[8]{0:T(128)} %param.12) | copy-start | bytes 100
  15.9 4.3 %copy-start.6 = (s32[8,1]{0,1:T(1,128)S(1)}, s32[8,1]{0,1:T(1,128)}, u32[]{:S(2)}) copy-start(s32[8,1]{0,1:T(1,128)} %param.11) | copy-start | bytes 100
  236.1 2.2 copy-start
  238.3 31.4 %copy-start.2 = (f32[1024]{0:T(1024)S(1)}, f32[1024]{0:T(1024)}, u32[]{:S(2)}) copy-start(f32[1024]{0:T(1024)} %param.16) | copy-start | bytes 12292
  269.7 21.7 %copy-start.3 = (f32[512]{0:T(512)S(1)}, f32[512]{0:T(512)}, u32[]{:S(2)}) copy-start(f32[512]{0:T(512)} %param.17) | copy-start | bytes 6148
Sparse Core Ops, SparseCore 0:
  37.8 198.2 reduce-scatter.1
where the time goes:
time: 302 us; the launch traced here: 301 us
  waiting for transfers between devices  198 us (66%)
  blocking collectives  51 us (17%)
  matrix products  30.4 us (10%)
  between operations  13.5 us (4%)
  other arithmetic  6 us (2%)
    reduce_scatter x1, waiting for transfers between devices, shards(): received = lax.psum_scatter(dense, 'dest', scatter_dimension=0, tiled=True)  198 us
    psum x1, blocking collectives, shards(): row_sums = lax.psum(jnp.sum(table, axis=1), 'dest')  31.1 us
    psum x1, blocking collectives, shards(): col_sums = lax.psum(jnp.sum(scaled, axis=0), 'orig')  19.9 us
    dot_general x1, matrix products, shards(): jnp.einsum('pb,bkl->pkl', picker, aggregated, preferred_element_type=jnp....  17.4 us
    dot_general x1, matrix products, shards(): jnp.einsum('sk,bsj->bkj', concord, root_blocks, preferred_element_type=jn...  8.7 us
  transfers between devices with their start and end apart: 1, of which 1 were waited for; matrix products, arithmetic and copies ran while one was open for 0% of the time, Pallas kernels for 0%

commit v1 on v0

v1 whole, which is shorter than its diff:
```python
import functools

import jax
import jax.numpy as jnp
from jax import lax
from jax.experimental import pallas as pl
from jax.experimental.pallas import tpu as pltpu
from jax.sharding import PartitionSpec as P

S_T = 128
HALF = S_T // 2
CAP = 2
SIDE = 4
MESH = pl.DeviceIdType.MESH
NT = (((1,), (1,)), ((), ()))
EXACT = lax.Precision.HIGHEST
F32 = jnp.float32
I32 = jnp.int32


def split(x):
    high = x.astype(jnp.bfloat16)
    return high, (x - high.astype(F32)).astype(jnp.bfloat16)


def route_kernel(
    sector_ref,
    owner,
    local_row,
    local_col,
    present,
    row_target,
    col_target,
    root,
    prior,
    got_a,
    got_b,
    meta_out,
    row_factor,
    col_factor,
    raw,
    concord_t,
    table,
    a_0,
    a_1,
    a_2,
    a_3,
    b_0,
    b_1,
    b_2,
    b_3,
    pack_a,
    pack_b,
    meta_v,
    meta_s,
    rows_1,
    rows_2,
    parts,
    cols_1,
    cols_2s,
    cols_2,
    cols_3,
    raw_sem,
    table_sem,
    meta_sem,
    gather_send,
    gather_recv,
    slot_send,
    slot_recv,
    keep_sem,
    small_send,
    small_recv,
    orig_send,
    orig_recv,
):
    from_a = (a_0, a_1, a_2, a_3)
    from_b = (b_0, b_1, b_2, b_3)
    n_blocks = root.shape[0]
    n_root = root.shape[1]
    n_orig = lax.axis_size("orig")
    tro = table.shape[0] // S_T
    trd = table.shape[1] // S_T
    o = lax.axis_index("orig")
    d = lax.axis_index("dest")
    y = d // SIDE
    z = d % SIDE

    def along_y(k):
        return (o, ((y + k) % SIDE) * SIDE + z)

    def along_z(k):
        return (o, y * SIDE + (z + k) % SIDE)

    def along_o(k):
        return ((o + k) % n_orig, d)

    def remote(src, dst, send, recv, device):
        return pltpu.make_async_remote_copy(
            src_ref=src, dst_ref=dst, send_sem=send, recv_sem=recv, device_id=device, device_id_type=MESH
        )

    def raw_copy(b):
        return pltpu.make_async_copy(root.at[b], raw.at[b], raw_sem.at[b])

    def start_raw(b, carry):
        raw_copy(b).start()
        return carry

    lax.fori_loop(0, n_blocks, start_raw, 0)
    table_copy = pltpu.make_async_copy(prior, table, table_sem)
    table_copy.start()

    barrier = pltpu.get_barrier_semaphore()
    for k in range(1, SIDE):
        pl.semaphore_signal(barrier, inc=1, device_id=along_y(k), device_id_type=MESH)
        pl.semaphore_signal(barrier, inc=1, device_id=along_z(k), device_id_type=MESH)
    for k in range(1, n_orig):
        pl.semaphore_signal(barrier, inc=1, device_id=along_o(k), device_id_type=MESH)

    target = lax.broadcasted_iota(I32, (S_T, S_T), 0)
    for c in range(n_root // S_T):
        concord_t[:, c * S_T : (c + 1) * S_T] = (target == sector_ref[c : c + 1, :]).astype(F32).astype(jnp.bfloat16)

    lane = lax.broadcasted_iota(I32, (1, S_T), 1)
    to = lane % 16
    kind = lane // 16
    none = jnp.full((1, S_T), tro * trd, I32)
    first = jnp.zeros((1, S_T), I32)
    second = jnp.zeros((1, S_T), I32)
    cell_1 = none
    cell_2 = none
    for b in reversed(range(n_blocks)):
        hit = to == owner[b, 0]
        second = jnp.where(hit, first, second)
        cell_2 = jnp.where(hit, cell_1, cell_2)
        first = jnp.where(hit, b, first)
        cell_1 = jnp.where(hit, local_row[b] * trd + local_col[b], cell_1)
    meta_v[z, y] = jnp.where(kind == 0, first, jnp.where(kind == 1, second, jnp.where(kind == 2, cell_1, cell_2)))

    pl.semaphore_wait(barrier, 2 * (SIDE - 1) + n_orig - 1)

    def small(i, k, src, dst, device):
        return remote(src, dst, small_send.at[i, k - 1], small_recv.at[i, k - 1], device)

    def meta_y(k):
        return small(0, k, meta_v.at[z, y], meta_v.at[z, y], along_y(k))

    def meta_z(k):
        return small(1, k, meta_v.at[z], meta_v.at[z], along_z(k))

    for k in range(1, SIDE):
        meta_y(k).start()

    def gather_copy(h, k, b):
        held, device = (from_a, along_y(k)) if h == 0 else (from_b, along_z(k))
        return remote(held[0].at[b], held[k].at[b], gather_send.at[h, k - 1, b], gather_recv.at[h, k - 1, b], device)

    sub = lax.broadcasted_iota(I32, (tro, S_T), 0)
    ones = jnp.ones((tro, S_T), F32)
    rows_1[y] = jnp.zeros((tro, S_T), F32)

    def aggregate(b, carry):
        raw_copy(b).wait()
        left = jnp.dot(concord_t[...], raw[b], preferred_element_type=F32)
        high, low = split(left)
        both = lax.dot_general(
            jnp.concatenate([high, low], axis=0), concord_t[...], NT, preferred_element_type=F32
        )
        block = (both[:S_T] + both[S_T:]) * present[b].astype(F32)
        a_0[b] = block[:HALF]
        b_0[b] = block[HALF:]
        for k in (2, 1, 3):
            gather_copy(0, k, b).start()
            gather_copy(1, k, b).start()
        sums = lax.dot_general(ones, block, NT, preferred_element_type=F32, precision=EXACT)
        rows_1[y] += jnp.where(sub == local_row[b], sums, 0.0)

        @pl.when(b == 2)
        def _():
            for k in range(1, SIDE):
                meta_y(k).wait()
            for k in range(1, SIDE):
                meta_z(k).start()

        return carry

    lax.fori_loop(0, n_blocks, aggregate, 0)

    for k in range(1, SIDE):
        meta_z(k).wait()
    meta_copy = pltpu.make_async_copy(meta_v, meta_s, meta_sem)
    meta_copy.start()
    meta_copy.wait()
    meta_out[...] = meta_v[...]

    def slot_copy(h, k, j):
        if h == 0:
            src, dst, device = pack_a.at[k, j], got_a.at[z, (y - j + SIDE) % SIDE], along_z(k)
        else:
            src, dst, device = pack_b.at[k, j], got_b.at[y, (z - j + SIDE) % SIDE], along_y(k)
        if k == 0:
            return pltpu.make_async_copy(src, dst, keep_sem.at[h, j])
        return remote(src, dst, slot_send.at[h, k - 1, j], slot_recv.at[h, k - 1, j], device)

    def fill(h, j):
        for k in (2, 1, 3, 0):
            for s in range(CAP):
                if h == 0:
                    source = (y - j + SIDE) % SIDE
                    index = meta_s[z, source, 0, y * SIDE + (z + k) % SIDE + 16 * s]
                    pack_a[k, j, s] = from_a[j][index]
                else:
                    source = (z - j + SIDE) % SIDE
                    index = meta_s[source, y, 0, ((y + k) % SIDE) * SIDE + z + 16 * s]
                    pack_b[k, j, s] = from_b[j][index]
            slot_copy(h, k, j).start()

    def arrived(j):
        def one(b, carry):
            gather_copy(0, j, b).wait_recv()
            gather_copy(1, j, b).wait_recv()
            return carry

        lax.fori_loop(0, n_blocks, one, 0)

    fill(0, 0)
    fill(1, 0)

    table_copy.wait()

    def prior_rows(r, carry):
        at = pl.multiple_of(r * S_T, S_T)
        tile = table[pl.ds(at, S_T), 0:S_T]
        for c in range(1, trd):
            tile += table[pl.ds(at, S_T), c * S_T : (c + 1) * S_T]
        sums = lax.dot_general(ones, tile, NT, preferred_element_type=F32, precision=EXACT)
        rows_1[y] += jnp.where(sub == r, sums, 0.0)
        return carry

    lax.fori_loop(0, tro, prior_rows, 0)

    def rows_y(k):
        return small(2, k, rows_1.at[y], rows_1.at[y], along_y(k))

    def rows_z(k):
        return small(3, k, rows_2.at[z], rows_2.at[z], along_z(k))

    for k in range(1, SIDE):
        rows_y(k).start()
    arrived(1)
    fill(0, 1)
    fill(1, 1)
    for k in range(1, SIDE):
        rows_y(k).wait()
    rows_2[z] = (rows_1[0] + rows_1[1]) + (rows_1[2] + rows_1[3])
    for k in range(1, SIDE):
        rows_z(k).start()
    arrived(3)
    fill(0, 3)
    fill(1, 3)
    for k in range(1, SIDE):
        rows_z(k).wait()
    factor = row_target[...] / ((rows_2[0] + rows_2[1]) + (rows_2[2] + rows_2[3]))
    row_factor[...] = factor

    parts[...] = jnp.zeros_like(parts)
    place = lax.broadcasted_iota(I32, parts.shape, 0) * trd + lax.broadcasted_iota(I32, parts.shape, 1)

    def block_cols(b, carry):
        weight = jnp.where(sub == local_row[b], factor, 0.0)
        sums = jnp.dot(weight[:, :HALF], a_0[b], preferred_element_type=F32, precision=EXACT) + jnp.dot(
            weight[:, HALF:], b_0[b], preferred_element_type=F32, precision=EXACT
        )
        line = jnp.sum(sums, axis=0, keepdims=True)
        here = place == owner[b, 0] * trd + local_col[b]
        parts[...] += jnp.where(here, jnp.broadcast_to(line[None], parts.shape), 0.0)
        return carry

    lax.fori_loop(0, n_blocks, block_cols, 0)

    def cols_y(k):
        return small(4, k, parts.at[pl.ds(((y + k) % SIDE) * SIDE, SIDE)], cols_1.at[y], along_y(k))

    def cols_z(k):
        return small(5, k, cols_2s.at[(z + k) % SIDE], cols_2.at[z], along_z(k))

    for k in range(1, SIDE):
        cols_y(k).start()
    cols_1[y] = parts[pl.ds(y * SIDE, SIDE)]
    arrived(2)
    fill(0, 2)
    fill(1, 2)

    def prior_cols(r, carry):
        at = pl.multiple_of(r * S_T, S_T)
        weight = jnp.where(sub == r, factor, 0.0)
        return carry + jnp.dot(weight, table[pl.ds(at, S_T), :], preferred_element_type=F32, precision=EXACT)

    wide = lax.fori_loop(0, tro, prior_cols, jnp.zeros((tro, trd * S_T), F32))
    wide = jnp.sum(wide, axis=0, keepdims=True)

    for k in range(1, SIDE):
        cols_y(k).wait()
    cols_2s[...] = (cols_1[0] + cols_1[1]) + (cols_1[2] + cols_1[3])
    for k in range(1, SIDE):
        cols_z(k).start()
    cols_2[z] = cols_2s[z]
    for k in range(1, SIDE):
        cols_z(k).wait()
    moved = (cols_2[0] + cols_2[1]) + (cols_2[2] + cols_2[3])
    for c in range(trd):
        cols_3[o, c : c + 1, :] = moved[c : c + 1, :] + wide[:, c * S_T : (c + 1) * S_T]

    def cols_o(k):
        return remote(cols_3.at[o], cols_3.at[o], orig_send.at[k - 1], orig_recv.at[k - 1], along_o(k))

    for k in range(1, n_orig):
        cols_o(k).start()
    for k in range(1, n_orig):
        cols_o(k).wait()
    total = cols_3[0]
    for i in range(1, n_orig):
        total += cols_3[i]
    col_factor[...] = col_target[...] / total

    def sent(b, carry):
        for k in range(1, SIDE):
            gather_copy(0, k, b).wait_send()
            gather_copy(1, k, b).wait_send()
        return carry

    lax.fori_loop(0, n_blocks, sent, 0)
    for j in (0, 1, 3, 2):
        for k in (0, 1, 3, 2):
            slot_copy(0, k, j).wait()
            slot_copy(1, k, j).wait()


def place_kernel(meta, row_factor, col_factor, got_a, got_b, prior, out, table, slots_a, slots_b, sem, out_sem):
    trd = table.shape[1] // S_T
    tro = table.shape[0] // S_T
    me = lax.axis_index("dest")
    copies = [
        pltpu.make_async_copy(prior, table, sem.at[0]),
        pltpu.make_async_copy(got_a, slots_a, sem.at[1]),
        pltpu.make_async_copy(got_b, slots_b, sem.at[2]),
    ]
    for copy in copies:
        copy.start()
    for copy in copies:
        copy.wait()

    def add(i, carry):
        ys = i // SIDE
        zs = i % SIDE
        for s in range(CAP):
            cell = meta[zs, ys, 0, me + 16 * (2 + s)]

            @pl.when(cell < tro * trd)
            def _():
                at = pl.multiple_of((cell // trd) * S_T, S_T)
                col = pl.multiple_of((cell % trd) * S_T, S_T)
                table[pl.ds(at, HALF), pl.ds(col, S_T)] += slots_a[zs, ys, s]
                table[pl.ds(at + HALF, HALF), pl.ds(col, S_T)] += slots_b[ys, zs, s]

        return carry

    lax.fori_loop(0, SIDE * SIDE, add, 0)

    def out_copy(r):
        at = pl.multiple_of(r * S_T, S_T)
        return pltpu.make_async_copy(table.at[pl.ds(at, S_T)], out.at[pl.ds(at, S_T)], out_sem.at[r])

    for r in range(tro):
        scale = jnp.transpose(jnp.broadcast_to(row_factor[r : r + 1, :], (S_T, S_T)))
        for c in range(trd):
            where = (slice(r * S_T, (r + 1) * S_T), slice(c * S_T, (c + 1) * S_T))
            table[where] = (scale * table[where]) * col_factor[c : c + 1, :]
        out_copy(r).start()
    for r in range(tro):
        out_copy(r).wait()


def shards(
    root_blocks,
    sector_map,
    dest_owner,
    local_row,
    local_col,
    present,
    prior,
    row_target,
    col_target,
):
    n_blocks, n_root, _ = root_blocks.shape
    rows_here, cols_here = prior.shape
    tro = rows_here // S_T
    trd = cols_here // S_T
    n_orig = lax.axis_size("orig")
    vmem = pl.BlockSpec(memory_space=pltpu.VMEM)
    smem = pl.BlockSpec(memory_space=pltpu.SMEM)
    hbm = pl.BlockSpec(memory_space=pl.ANY)
    dma = pltpu.SemaphoreType.DMA
    got = jax.ShapeDtypeStruct((SIDE, SIDE, CAP, HALF, S_T), F32)
    got_a, got_b, meta, row_factor, col_factor = pl.pallas_call(
        route_kernel,
        out_shape=(
            got,
            got,
            jax.ShapeDtypeStruct((SIDE, SIDE, 1, S_T), I32),
            jax.ShapeDtypeStruct((tro, S_T), F32),
            jax.ShapeDtypeStruct((trd, S_T), F32),
        ),
        in_specs=[vmem, smem, smem, smem, smem, vmem, vmem, hbm, hbm],
        out_specs=(hbm, hbm, vmem, vmem, vmem),
        scratch_shapes=[
            pltpu.VMEM((n_blocks, n_root, n_root), jnp.bfloat16),
            pltpu.VMEM((S_T, n_root), jnp.bfloat16),
            pltpu.VMEM((rows_here, cols_here), F32),
            *[pltpu.VMEM((n_blocks, HALF, S_T), F32)] * (2 * SIDE),
            pltpu.VMEM((SIDE, SIDE, CAP, HALF, S_T), F32),
            pltpu.VMEM((SIDE, SIDE, CAP, HALF, S_T), F32),
            pltpu.VMEM((SIDE, SIDE, 1, S_T), I32),
            pltpu.SMEM((SIDE, SIDE, 1, S_T), I32),
            pltpu.VMEM((SIDE, tro, S_T), F32),
            pltpu.VMEM((SIDE, tro, S_T), F32),
            pltpu.VMEM((SIDE * SIDE, trd, S_T), F32),
            pltpu.VMEM((SIDE, SIDE, trd, S_T), F32),
            pltpu.VMEM((SIDE, trd, S_T), F32),
            pltpu.VMEM((SIDE, trd, S_T), F32),
            pltpu.VMEM((n_orig, trd, S_T), F32),
            dma((n_blocks,)),
            dma,
            dma,
            dma((2, SIDE - 1, n_blocks)),
            dma((2, SIDE - 1, n_blocks)),
            dma((2, SIDE - 1, SIDE)),
            dma((2, SIDE - 1, SIDE)),
            dma((2, SIDE)),
            dma((6, SIDE - 1)),
            dma((6, SIDE - 1)),
            dma((n_orig - 1,)),
            dma((n_orig - 1,)),
        ],
        compiler_params=pltpu.CompilerParams(
            collective_id=0, has_side_effects=True, vmem_limit_bytes=48 << 20
        ),
        name="route",
    )(
        sector_map.reshape(n_root // S_T, S_T),
        dest_owner,
        local_row,
        local_col,
        present,
        row_target.reshape(tro, S_T),
        col_target.reshape(trd, S_T),
        root_blocks,
        prior,
    )
    return pl.pallas_call(
        place_kernel,
        out_shape=jax.ShapeDtypeStruct((rows_here, cols_here), F32),
        in_specs=[smem, vmem, vmem, hbm, hbm, hbm],
        out_specs=hbm,
        scratch_shapes=[
            pltpu.VMEM((rows_here, cols_here), F32),
            pltpu.VMEM((SIDE, SIDE, CAP, HALF, S_T), F32),
            pltpu.VMEM((SIDE, SIDE, CAP, HALF, S_T), F32),
            dma((3,)),
            dma((tro,)),
        ],
        compiler_params=pltpu.CompilerParams(vmem_limit_bytes=24 << 20),
        name="place",
    )(meta, row_factor, col_factor, got_a, got_b, prior)


def solution(mesh):
    placed = (
        P(("orig", "dest"), None, None),
        P(),
        P(("orig", "dest"), None),
        P(("orig", "dest")),
        P(("orig", "dest")),
        P(("orig", "dest")),
        P("orig", "dest"),
        P("orig"),
        P("dest"),
    )
    return jax.shard_map(
        shards, mesh=mesh, in_specs=placed, out_specs=P("orig", "dest"), check_vma=False
    )
```

time: 302 us -> 54.4 us (0.18)
  waiting for transfers between devices: 198 us -> 0 us
  blocking collectives: 51 us -> 0 us
  Pallas kernels: 0 us -> 47.8 us
  matrix products: 30.4 us -> 0 us
  between operations: 13.5 us -> 0.02 us
  other arithmetic: 6 us -> 0 us
  local copies, waits for them, and re-layouts: 2.25 us -> 6.34 us
    reduce_scatter x1 -> x0, waiting for transfers between devices: 198 us -> none  [shards(): received = lax.psum_scatter(dense, 'dest', scatter_dimension=0, tiled=True)]
    psum x2 -> x0, blocking collectives: 51 us -> none  [the longest x1 31.1 us: shards(): row_sums = lax.psum(jnp.sum(table, axis=1), 'dest')]
    pallas_call x0 -> x2, Pallas kernels: none -> 47.8 us  [the longest x1 44.6 us: shards(): pl.pallas_call(route_kernel, out_shape=(got, got, jax.ShapeDtypeStruct((S...]
    dot_general x3 -> x0, matrix products: 30.4 us -> none  [the longest x1 17.4 us: shards(): jnp.einsum('pb,bkl->pkl', picker, aggregated, preferred_element_type=jnp....]
    unnamed x14 -> x15, local copies, waits for them, and re-layouts: 0.13 us -> 6.34 us
    mul x1 -> x0, other arithmetic: 3.2 us -> none  [shards(): return scaled * col_factor[None, :]]
  transfers between devices with their start and end apart: 1 -> 0, of which waited for: 1 -> 0; matrix products, arithmetic and copies ran while one was open for 0% -> 0% of each run, Pallas kernels for 0% -> 0%
where the time goes in v1:
time: 54.4 us; the launch traced here: 54.1 us
  Pallas kernels  47.8 us (88%)
  local copies, waits for them, and re-layouts  6.34 us (12%)
    pallas_call x1, Pallas kernels, shards(): pl.pallas_call(route_kernel, out_shape=(got, got, jax.ShapeDtypeStruct((S...  44.6 us
    unnamed x15, local copies, waits for them, and re-layouts  6.34 us
    pallas_call x1, Pallas kernels, shards(): pl.pallas_call(place_kernel, out_shape=jax.ShapeDtypeStruct((rows_here, c...  3.16 us

profile of v1, /device:TPU:1, one launch (start us, length us, event | category | flops | bytes accessed | tf_op | source)
XLA Modules:
  0.0 54.1 jit_solution(12146112880676656584)
XLA Ops:
  0.0 0.7 %copy.10.owner = s32[8,1]{1,0:T(8,128)S(1)} copy(s32[8,1]{0,1:T(1,128)} %param.11) | data formatting | bytes 64 | tf_op args[2]
  0.7 0.0 copy-start
  0.7 1.6 %copy-done = f32[1024,512]{1,0:T(8,128)S(1)} copy-done((f32[1024,512]{1,0:T(8,128)S(1)}, f32[1024,512]{1,0:T(8,128)}, u32[]{:S(2)}) %copy-start) | copy-done | bytes 2097176
  2.3 0.0 copy-start.1
  2.3 0.7 %copy-done.1 = s32[1024]{0:T(1024)S(1)} copy-done((s32[1024]{0:T(1024)S(1)}, s32[1024]{0:T(1024)}, u32[]{:S(2)}) %copy-start.1) | copy-done | bytes 4120
  3.0 0.0 copy-start.2
  3.0 0.7 %copy-done.2 = f32[1024]{0:T(1024)S(1)} copy-done((f32[1024]{0:T(1024)S(1)}, f32[1024]{0:T(1024)}, u32[]{:S(2)}) %copy-start.2) | copy-done | bytes 4120
  3.7 0.0 copy-start.3
  3.7 0.7 %copy-done.3 = f32[512]{0:T(512)S(1)} copy-done((f32[512]{0:T(512)S(1)}, f32[512]{0:T(512)}, u32[]{:S(2)}) %copy-start.3) | copy-done | bytes 2072
  4.4 0.0 copy-start.4
  4.4 0.7 %copy-done.4 = s32[8]{0:T(128)S(1)} copy-done((s32[8]{0:T(128)S(1)}, s32[8]{0:T(128)}, u32[]{:S(2)}) %copy-start.4) | copy-done | bytes 56
  5.0 0.0 copy-start.5
  5.0 0.7 %copy-done.5 = s32[8]{0:T(128)S(1)} copy-done((s32[8]{0:T(128)S(1)}, s32[8]{0:T(128)}, u32[]{:S(2)}) %copy-start.5) | copy-done | bytes 56
  5.7 0.0 copy-start.6
  5.7 0.7 %copy-done.6 = s32[8]{0:T(128)S(1)} copy-done((s32[8]{0:T(128)S(1)}, s32[8]{0:T(128)}, u32[]{:S(2)}) %copy-start.6) | copy-done | bytes 56
  6.3 44.6 %route.1 = (f32[4,4,2,64,128]{4,3,2,1,0:T(8,128)S(1)}, f32[4,4,2,64,128]{4,3,2,1,0:T(8,128)S(1)}, s32[4,4,1,128]{3,2,1,0:T(1,128)S(1)}, f32[8,128]{1,0:T(8,128)S(1)}, f32[4,128]{1,0:T(4,128)S(1)}) custom-call(s32[8,128]{1,0:T(8,128)S(1)} %bitcast.3, s32[8,1]{1,0:T(8,128)S(1)} %copy.10.owner, s32[8]{0:T(128)S(1)} %copy-done.4, s32[8]{0:T(128)S(1)} %copy-done.5, ...), custom_call_target="tpu_custom_call" | custom-call | tf_op jit(solution)/shard_map/route/pallas_call | solution.py:405
  51.0 3.2 %place.1 = f32[1024,512]{1,0:T(8,128)} custom-call(s32[4,4,1,128]{3,2,1,0:T(1,128)S(1)} %get-tuple-element.10.meta, f32[8,128]{1,0:T(8,128)S(1)} %get-tuple-element.11.row_factor, f32[4,128]{1,0:T(4,128)S(1)} %get-tuple-element.12.col_factor, f32[4,4,2,64,128]{4,3,2,1,0:T(8,128)S(1)} %get-tuple-element.13.got_a, ...), custom_call_target="tpu_custom_call" | custom-call | tf_op jit(solution)/shard_map/place/pallas_call | solution.py:460
Async XLA Ops:
  0.7 1.6 %copy-start = (f32[1024,512]{1,0:T(8,128)S(1)}, f32[1024,512]{1,0:T(8,128)}, u32[]{:S(2)}) copy-start(f32[1024,512]{1,0:T(8,128)} %prior.3) | copy-start | bytes 6291460
  2.3 0.7 %copy-start.1 = (s32[1024]{0:T(1024)S(1)}, s32[1024]{0:T(1024)}, u32[]{:S(2)}) copy-start(s32[1024]{0:T(1024)} %param.10) | copy-start | bytes 12292
  3.0 0.7 %copy-start.2 = (f32[1024]{0:T(1024)S(1)}, f32[1024]{0:T(1024)}, u32[]{:S(2)}) copy-start(f32[1024]{0:T(1024)} %param.16) | copy-start | bytes 12292
  3.7 0.7 %copy-start.3 = (f32[512]{0:T(512)S(1)}, f32[512]{0:T(512)}, u32[]{:S(2)}) copy-start(f32[512]{0:T(512)} %param.17) | copy-start | bytes 6148
  4.4 0.7 %copy-start.4 = (s32[8]{0:T(128)S(1)}, s32[8]{0:T(128)}, u32[]{:S(2)}) copy-start(s32[8]{0:T(128)} %local_row.1) | copy-start | bytes 100
  5.0 0.7 %copy-start.5 = (s32[8]{0:T(128)S(1)}, s32[8]{0:T(128)}, u32[]{:S(2)}) copy-start(s32[8]{0:T(128)} %local_col.1) | copy-start | bytes 100
  5.7 0.7 %copy-start.6 = (s32[8]{0:T(128)S(1)}, s32[8]{0:T(128)}, u32[]{:S(2)}) copy-start(s32[8]{0:T(128)} %present.1) | copy-start | bytes 100

commit v2 on v1

v2 whole, which is shorter than its diff:
```python
import functools

import jax
import jax.numpy as jnp
from jax import lax
from jax.experimental import pallas as pl
from jax.experimental.pallas import tpu as pltpu
from jax.sharding import PartitionSpec as P

S_T = 128
HALF = S_T // 2
CAP = 2
SIDE = 4
LAG = 5
LATE = 5
MESH = pl.DeviceIdType.MESH
NT = (((1,), (1,)), ((), ()))
F32 = jnp.float32
I32 = jnp.int32


def split(x):
    high = x.astype(jnp.bfloat16)
    return high, (x - high.astype(F32)).astype(jnp.bfloat16)


def route_kernel(
    sector_hbm,
    owner_hbm,
    local_row_hbm,
    local_col_hbm,
    present_hbm,
    row_target_hbm,
    col_target_hbm,
    root,
    prior,
    got_a,
    got_b,
    meta_out,
    weights,
    table,
    col_factor,
    sector_ref,
    owner,
    local_row,
    local_col,
    present,
    row_target,
    col_target,
    raw,
    concord_t,
    a_0,
    a_1,
    a_2,
    a_3,
    b_0,
    b_1,
    b_2,
    b_3,
    pack_a,
    pack_b,
    meta_v,
    meta_s,
    row_acc,
    rows,
    cols_a,
    cols_b,
    cols_all,
    small_sem,
    raw_sem,
    table_sem,
    meta_sem,
    gather_send,
    gather_recv,
    pass_send,
    pass_recv,
    slot_send,
    slot_recv,
    keep_sem,
    small_send,
    small_recv,
    rows_send,
    rows_recv,
    cols_send,
    cols_recv,
    orig_send,
    orig_recv,
):
    from_a = (a_0, a_1, a_2, a_3)
    from_b = (b_0, b_1, b_2, b_3)
    n_blocks = root.shape[0]
    n_root = root.shape[1]
    n_orig = lax.axis_size("orig")
    n_dest = lax.axis_size("dest")
    tro = table.shape[0] // S_T
    trd = table.shape[1] // S_T
    o = lax.axis_index("orig")
    d = lax.axis_index("dest")
    y = d // SIDE
    z = d % SIDE

    def along_y(k):
        return (o, ((y + k) % SIDE) * SIDE + z)

    def along_z(k):
        return (o, y * SIDE + (z + k) % SIDE)

    def along_d(i):
        return (o, (d + i) % n_dest)

    def along_o(k):
        return ((o + k) % n_orig, d)

    def remote(src, dst, send, recv, device):
        return pltpu.make_async_remote_copy(
            src_ref=src, dst_ref=dst, send_sem=send, recv_sem=recv, device_id=device, device_id_type=MESH
        )

    def raw_copy(b):
        return pltpu.make_async_copy(root.at[b], raw.at[b], raw_sem.at[b])

    barrier = pltpu.get_barrier_semaphore()
    for k in range(1, SIDE):
        pl.semaphore_signal(barrier, inc=1, device_id=along_y(k), device_id_type=MESH)
        pl.semaphore_signal(barrier, inc=1, device_id=along_z(k), device_id_type=MESH)
    for k in range(1, n_orig):
        pl.semaphore_signal(barrier, inc=1, device_id=along_o(k), device_id_type=MESH)

    loads = [
        pltpu.make_async_copy(src, dst, small_sem.at[i])
        for i, (src, dst) in enumerate(
            (
                (sector_hbm, sector_ref),
                (owner_hbm, owner),
                (local_row_hbm, local_row),
                (local_col_hbm, local_col),
                (present_hbm, present),
                (row_target_hbm, row_target),
                (col_target_hbm, col_target),
            )
        )
    ]
    for load in loads:
        load.start()

    def start_raw(b, carry):
        raw_copy(b).start()
        return carry

    lax.fori_loop(0, n_blocks, start_raw, 0)
    table_copy = pltpu.make_async_copy(prior, table, table_sem)

    for load in loads:
        load.wait()

    target = lax.broadcasted_iota(I32, (S_T, S_T), 0)
    for c in range(n_root // S_T):
        concord_t[:, c * S_T : (c + 1) * S_T] = (target == sector_ref[c : c + 1, :]).astype(F32).astype(jnp.bfloat16)

    lane = lax.broadcasted_iota(I32, (1, S_T), 1)
    to = lane % 16
    kind = lane // 16
    none = jnp.full((1, S_T), tro * trd, I32)
    first = jnp.zeros((1, S_T), I32)
    second = jnp.zeros((1, S_T), I32)
    cell_1 = none
    cell_2 = none
    for b in reversed(range(n_blocks)):
        hit = to == owner[0, b]
        second = jnp.where(hit, first, second)
        cell_2 = jnp.where(hit, cell_1, cell_2)
        first = jnp.where(hit, b, first)
        cell_1 = jnp.where(hit, local_row[0, b] * trd + local_col[0, b], cell_1)
    meta_v[z, y] = jnp.where(kind == 0, first, jnp.where(kind == 1, second, jnp.where(kind == 2, cell_1, cell_2)))

    pl.semaphore_wait(barrier, 2 * (SIDE - 1) + n_orig - 1)

    def small(i, k, src, dst, device):
        return remote(src, dst, small_send.at[i, k - 1], small_recv.at[i, k - 1], device)

    def meta_y(k):
        return small(0, k, meta_v.at[z, y], meta_v.at[z, y], along_y(k))

    def meta_z(k):
        return small(1, k, meta_v.at[z], meta_v.at[z], along_z(k))

    for k in range(1, SIDE):
        meta_y(k).start()

    def gather_copy(h, k, b):
        held, device = (from_a, along_y(k)) if h == 0 else (from_b, along_z(k))
        return remote(held[0].at[b], held[k].at[b], gather_send.at[h, k - 1, b], gather_recv.at[h, k - 1, b], device)

    def pass_copy(h, way, b):
        held = from_a if h == 0 else from_b
        along = along_y if h == 0 else along_z
        piece = pl.ds(0, HALF // 2) if way == 0 else pl.ds(HALF // 2, HALF // 2)
        source, k = (1, 1) if way == 0 else (3, 3)
        return remote(
            held[source].at[b, piece],
            held[2].at[b, piece],
            pass_send.at[h, way, b],
            pass_recv.at[h, way, b],
            along(k),
        )

    def forward(b):
        for way, k in ((0, 1), (1, 3)):
            for h in (0, 1):
                gather_copy(h, k, b).wait_recv()
                pass_copy(h, way, b).start()

    lanes = lax.broadcasted_iota(I32, (S_T, S_T), 1)
    row_acc[...] = jnp.zeros_like(row_acc)

    def aggregate(b, carry):
        raw_copy(b).wait()

        @pl.when(b == LATE)
        def _():
            table_copy.start()

        left = jnp.dot(concord_t[...], raw[b], preferred_element_type=F32)
        high, low = split(left)
        both = lax.dot_general(
            jnp.concatenate([high, low], axis=0), concord_t[...], NT, preferred_element_type=F32
        )
        block = (both[:S_T] + both[S_T:]) * present[0, b].astype(F32)
        a_0[b] = block[:HALF]
        b_0[b] = block[HALF:]
        for k in (1, 3):
            gather_copy(0, k, b).start()
            gather_copy(1, k, b).start()

        @pl.when(b >= LAG)
        def _():
            forward(b - LAG)

        sums = jnp.sum(block, axis=1, keepdims=True)
        row_acc[...] += jnp.where(lanes == local_row[0, b], sums, 0.0)

        @pl.when(b == 2)
        def _():
            for k in range(1, SIDE):
                meta_y(k).wait()
            for k in range(1, SIDE):
                meta_z(k).start()

        return carry

    lax.fori_loop(0, n_blocks, aggregate, 0)

    table_copy.wait()

    def prior_rows(r, carry):
        at = pl.multiple_of(r * S_T, S_T)
        tile = table[pl.ds(at, S_T), 0:S_T]
        for c in range(1, trd):
            tile += table[pl.ds(at, S_T), c * S_T : (c + 1) * S_T]
        row_acc[...] += jnp.where(lanes == r, jnp.sum(tile, axis=1, keepdims=True), 0.0)
        return carry

    lax.fori_loop(0, tro, prior_rows, 0)
    rows[d] = jnp.transpose(row_acc[...])[:tro]

    def rows_copy(i):
        return remote(rows.at[d], rows.at[d], rows_send.at[i - 1], rows_recv.at[i - 1], along_d(i))

    def start_rows(i, carry):
        rows_copy(i).start()
        return carry

    lax.fori_loop(1, n_dest, start_rows, 0)

    for k in range(1, SIDE):
        meta_z(k).wait()
    meta_copy = pltpu.make_async_copy(meta_v, meta_s, meta_sem)
    meta_copy.start()
    meta_copy.wait()
    meta_out[...] = meta_v[...]

    def slot_copy(h, k, j):
        if h == 0:
            src, dst, device = pack_a.at[k, j], got_a.at[z, (y - j + SIDE) % SIDE], along_z(k)
        else:
            src, dst, device = pack_b.at[k, j], got_b.at[y, (z - j + SIDE) % SIDE], along_y(k)
        if k == 0:
            return pltpu.make_async_copy(src, dst, keep_sem.at[h, j])
        return remote(src, dst, slot_send.at[h, k - 1, j], slot_recv.at[h, k - 1, j], device)

    def fill(h, j):
        for k in (2, 1, 3, 0):
            for s in range(CAP):
                if h == 0:
                    source = (y - j + SIDE) % SIDE
                    index = meta_s[z, source, 0, y * SIDE + (z + k) % SIDE + 16 * s]
                    pack_a[k, j, s] = from_a[j][index]
                else:
                    source = (z - j + SIDE) % SIDE
                    index = meta_s[source, y, 0, ((y + k) % SIDE) * SIDE + z + 16 * s]
                    pack_b[k, j, s] = from_b[j][index]

    def send(h, j):
        for k in (2, 1, 3, 0):
            slot_copy(h, k, j).start()

    fill(0, 0)
    send(0, 0)
    fill(1, 0)
    send(1, 0)

    def late(b, carry):
        forward(b)
        return carry

    lax.fori_loop(n_blocks - LAG, n_blocks, late, 0)

    fill(0, 1)
    send(0, 1)
    fill(1, 1)
    send(1, 1)
    fill(0, 3)
    fill(1, 3)

    def passed(b, carry):
        for way in (0, 1):
            pass_copy(0, way, b).wait_recv()
            pass_copy(1, way, b).wait_recv()
        return carry

    lax.fori_loop(0, n_blocks, passed, 0)
    fill(0, 2)
    fill(1, 2)

    def wait_rows(i, carry):
        rows_copy(i).wait()
        return carry

    lax.fori_loop(1, n_dest, wait_rows, 0)
    total = rows[0]
    for i in range(1, n_dest):
        total += rows[i]
    factor = row_target[...] / total
    upright = jnp.transpose(jnp.concatenate([factor, jnp.zeros((S_T - tro, S_T), F32)], axis=0))
    for r in range(tro):
        weights[r] = jnp.broadcast_to(upright[:, r : r + 1], (S_T, S_T))

    col_of = lax.broadcasted_iota(I32, (trd, S_T), 0)

    def line_cols(i, carry):
        s = i % CAP
        sums = list(carry)
        for j in range(SIDE):
            for h in (0, 1):
                for k in range(SIDE):
                    if h == 0:
                        cell = meta_s[z, (y - j + SIDE) % SIDE, 0, y * SIDE + (z + k) % SIDE + 16 * (2 + s)]
                        slot = pack_a[k, j, s]
                    else:
                        cell = meta_s[(z - j + SIDE) % SIDE, y, 0, ((y + k) % SIDE) * SIDE + z + 16 * (2 + s)]
                        slot = pack_b[k, j, s]
                    weight = weights[jnp.minimum(cell // trd, tro - 1), h * HALF : (h + 1) * HALF]
                    line = jnp.sum(weight * slot, axis=0, keepdims=True)
                    column = jnp.where(cell < tro * trd, cell % trd, trd)
                    sums[h * SIDE + k] += jnp.where(col_of == column, line, 0.0)
        return tuple(sums)

    nothing = jnp.zeros((trd, S_T), F32)
    sums = lax.fori_loop(0, CAP, line_cols, (nothing,) * (2 * SIDE))
    for k in range(SIDE):
        cols_a[k] = sums[k]
        cols_b[k] = sums[SIDE + k]

    def cols_copy(h, k):
        held, along = (cols_a, along_z(k)) if h == 0 else (cols_b, along_y(k))
        return remote(held.at[k], held.at[SIDE + k], cols_send.at[h, k - 1], cols_recv.at[h, k - 1], along)

    for k in (2, 1, 3):
        cols_copy(0, k).start()
        cols_copy(1, k).start()
    send(0, 3)
    send(1, 3)
    send(0, 2)
    send(1, 2)

    def prior_cols(r, carry):
        at = pl.multiple_of(r * S_T, S_T)
        weight = weights[r]
        lines = [
            jnp.sum(weight * table[pl.ds(at, S_T), c * S_T : (c + 1) * S_T], axis=0, keepdims=True)
            for c in range(trd)
        ]
        return carry + jnp.concatenate(lines, axis=0)

    wide = lax.fori_loop(0, tro, prior_cols, jnp.zeros((trd, S_T), F32))

    wide += cols_a[0] + cols_b[0]
    for k in range(1, SIDE):
        cols_copy(0, k).wait()
        cols_copy(1, k).wait()
        wide += cols_a[SIDE + k] + cols_b[SIDE + k]
    cols_all[o] = wide

    def cols_o(k):
        return remote(cols_all.at[o], cols_all.at[o], orig_send.at[k - 1], orig_recv.at[k - 1], along_o(k))

    for k in range(1, n_orig):
        cols_o(k).start()
    for k in range(1, n_orig):
        cols_o(k).wait()
    total = cols_all[0]
    for i in range(1, n_orig):
        total += cols_all[i]
    col_factor[...] = col_target[...] / total

    def scale(r, carry):
        at = pl.multiple_of(r * S_T, S_T)
        for c in range(trd):
            columns = slice(c * S_T, (c + 1) * S_T)
            table[pl.ds(at, S_T), columns] = weights[r] * table[pl.ds(at, S_T), columns] * col_factor[c : c + 1, :]
        return carry

    lax.fori_loop(0, tro, scale, 0)

    def sent(b, carry):
        for h in (0, 1):
            for way, k in ((0, 1), (1, 3)):
                gather_copy(h, k, b).wait_send()
                pass_copy(h, way, b).wait_send()
        return carry

    lax.fori_loop(0, n_blocks, sent, 0)
    for j in (0, 1, 3, 2):
        for k in (0, 1, 3, 2):
            slot_copy(0, k, j).wait()
            slot_copy(1, k, j).wait()


def place_kernel(meta, weights, col_factor, slots_a, slots_b, table_in, out, table, out_sem):
    trd = table.shape[1] // S_T
    tro = table.shape[0] // S_T
    me = lax.axis_index("dest")

    def add(i, carry):
        ys = i // SIDE
        zs = i % SIDE
        for s in range(CAP):
            cell = meta[zs, ys, 0, me + 16 * (2 + s)]

            @pl.when(cell < tro * trd)
            def _():
                row = cell // trd
                at = pl.multiple_of(row * S_T, S_T)
                col = pl.multiple_of((cell % trd) * S_T, S_T)
                across = col_factor[pl.ds(cell % trd, 1), :]
                table[pl.ds(at, HALF), pl.ds(col, S_T)] += weights[row, :HALF] * slots_a[zs, ys, s] * across
                table[pl.ds(at + HALF, HALF), pl.ds(col, S_T)] += weights[row, HALF:] * slots_b[ys, zs, s] * across

        return carry

    lax.fori_loop(0, SIDE * SIDE, add, 0)

    def out_copy(r):
        at = pl.multiple_of(r * S_T, S_T)
        return pltpu.make_async_copy(table.at[pl.ds(at, S_T)], out.at[pl.ds(at, S_T)], out_sem.at[r])

    for r in range(tro):
        out_copy(r).start()
    for r in range(tro):
        out_copy(r).wait()


def shards(
    root_blocks,
    sector_map,
    dest_owner,
    local_row,
    local_col,
    present,
    prior,
    row_target,
    col_target,
):
    n_blocks, n_root, _ = root_blocks.shape
    rows_here, cols_here = prior.shape
    tro = rows_here // S_T
    trd = cols_here // S_T
    n_orig = lax.axis_size("orig")
    n_dest = lax.axis_size("dest")
    vmem = pl.BlockSpec(memory_space=pltpu.VMEM)
    smem = pl.BlockSpec(memory_space=pltpu.SMEM)
    hbm = pl.BlockSpec(memory_space=pltpu.HBM)
    dma = pltpu.SemaphoreType.DMA
    got = jax.ShapeDtypeStruct((SIDE, SIDE, CAP, HALF, S_T), F32)
    got_a, got_b, meta, weights, table, col_factor = pl.pallas_call(
        route_kernel,
        out_shape=(
            got,
            got,
            jax.ShapeDtypeStruct((SIDE, SIDE, 1, S_T), I32),
            jax.ShapeDtypeStruct((tro, S_T, S_T), F32),
            jax.ShapeDtypeStruct((rows_here, cols_here), F32),
            jax.ShapeDtypeStruct((trd, S_T), F32),
        ),
        in_specs=[hbm] * 9,
        out_specs=(vmem,) * 6,
        scratch_shapes=[
            pltpu.VMEM((n_root // S_T, S_T), I32),
            *[pltpu.SMEM((1, n_blocks), I32)] * 4,
            pltpu.VMEM((tro, S_T), F32),
            pltpu.VMEM((trd, S_T), F32),
            pltpu.VMEM((n_blocks, n_root, n_root), jnp.bfloat16),
            pltpu.VMEM((S_T, n_root), jnp.bfloat16),
            *[pltpu.VMEM((n_blocks, HALF, S_T), F32)] * (2 * SIDE),
            pltpu.VMEM((SIDE, SIDE, CAP, HALF, S_T), F32),
            pltpu.VMEM((SIDE, SIDE, CAP, HALF, S_T), F32),
            pltpu.VMEM((SIDE, SIDE, 1, S_T), I32),
            pltpu.SMEM((SIDE, SIDE, 1, S_T), I32),
            pltpu.VMEM((S_T, S_T), F32),
            pltpu.VMEM((n_dest, tro, S_T), F32),
            pltpu.VMEM((2 * SIDE, trd, S_T), F32),
            pltpu.VMEM((2 * SIDE, trd, S_T), F32),
            pltpu.VMEM((n_orig, trd, S_T), F32),
            dma((7,)),
            dma((n_blocks,)),
            dma,
            dma,
            dma((2, SIDE - 1, n_blocks)),
            dma((2, SIDE - 1, n_blocks)),
            dma((2, 2, n_blocks)),
            dma((2, 2, n_blocks)),
            dma((2, SIDE - 1, SIDE)),
            dma((2, SIDE - 1, SIDE)),
            dma((2, SIDE)),
            dma((2, SIDE - 1)),
            dma((2, SIDE - 1)),
            dma((n_dest - 1,)),
            dma((n_dest - 1,)),
            dma((2, SIDE - 1)),
            dma((2, SIDE - 1)),
            dma((n_orig - 1,)),
            dma((n_orig - 1,)),
        ],
        compiler_params=pltpu.CompilerParams(
            collective_id=0, has_side_effects=True, vmem_limit_bytes=40 << 20
        ),
        name="route",
    )(*[pltpu.with_memory_space_constraint(x, pltpu.HBM) for x in (
        sector_map.reshape(n_root // S_T, S_T),
        dest_owner.reshape(1, n_blocks),
        local_row.reshape(1, n_blocks),
        local_col.reshape(1, n_blocks),
        present.reshape(1, n_blocks),
        row_target.reshape(tro, S_T),
        col_target.reshape(trd, S_T),
        root_blocks,
        prior,)]
    )
    out, _ = pl.pallas_call(
        place_kernel,
        out_shape=(
            jax.ShapeDtypeStruct((rows_here, cols_here), F32),
            jax.ShapeDtypeStruct((rows_here, cols_here), F32),
        ),
        in_specs=[smem, vmem, vmem, vmem, vmem, vmem],
        out_specs=(hbm, vmem),
        scratch_shapes=[dma((tro,))],
        input_output_aliases={5: 1},
        compiler_params=pltpu.CompilerParams(vmem_limit_bytes=8 << 20),
        name="place",
    )(meta, weights, col_factor, got_a, got_b, table)
    return out


def solution(mesh):
    placed = (
        P(("orig", "dest"), None, None),
        P(),
        P(("orig", "dest"), None),
        P(("orig", "dest")),
        P(("orig", "dest")),
        P(("orig", "dest")),
        P("orig", "dest"),
        P("orig"),
        P("dest"),
    )
    return jax.shard_map(
        shards, mesh=mesh, in_specs=placed, out_specs=P("orig", "dest"), check_vma=False
    )
```

time: 54.4 us -> 39.9 us (0.73)
  Pallas kernels: 47.8 us -> 39.8 us
  local copies, waits for them, and re-layouts: 6.34 us -> 0 us
    pallas_call x1, Pallas kernels: 44.6 us -> 37.1 us  [shards(): pl.pallas_call(route_kernel, out_shape=(got, got, jax.ShapeDtypeStruct((S...]
    unnamed x15 -> x0, local copies, waits for them, and re-layouts: 6.34 us -> none
where the time goes in v2:
time: 39.9 us; the launch traced here: 39.8 us
  Pallas kernels  39.8 us (100%)
    pallas_call x1, Pallas kernels, shards(): pl.pallas_call(route_kernel, out_shape=(got, got, jax.ShapeDtypeStruct((S...  37.1 us
    pallas_call x1, Pallas kernels, shards(): pl.pallas_call(place_kernel, out_shape=(jax.ShapeDtypeStruct((rows_here,...  2.69 us

profile of v2, /device:TPU:1, one launch (start us, length us, event | category | flops | bytes accessed | tf_op | source)
XLA Modules:
  0.0 39.8 jit_solution(1057358798851487938)
XLA Ops:
  0.0 37.1 %route.1 = (f32[4,4,2,64,128]{4,3,2,1,0:T(8,128)S(1)}, f32[4,4,2,64,128]{4,3,2,1,0:T(8,128)S(1)}, s32[4,4,1,128]{3,2,1,0:T(1,128)S(1)}, f32[8,128,128]{2,1,0:T(8...) custom-call(s32[8,128]{1,0:T(8,128)} %bitcast.7, s32[1,8]{1,0:T(1,128)} %bitcast.10, s32[1,8]{1,0:T(1,128)} %bitcast.11, ...), custom_call_target="tpu_custom_call" | custom-call | tf_op jit(solution)/shard_map/route/pallas_call | solution.py:495
  37.1 2.7 %place.1 = (f32[1024,512]{1,0:T(8,128)}, f32[1024,512]{1,0:T(8,128)S(1)}) custom-call(s32[4,4,1,128]{3,2,1,0:T(1,128)S(1)} %get-tuple-element.12.meta, f32[8,128,128]{2,1,0:T(8,128)S(1)} %get-tuple-element.13.weights, f32[4,128]{1,0:T(4,128)S(1)} %get-tuple-element.14.col_factor, ...), custom_call_target="tpu_custom_call", output_to_operand_aliasing={{1}: (5, {})} | custom-call | tf_op jit(solution)/shard_map/place/pallas_call | solution.py:559

commit v3 on v2

--- a/solution.py
+++ b/solution.py
@@ -11,8 +11,7 @@
 HALF = S_T // 2
 CAP = 2
 SIDE = 4
-LAG = 5
-LATE = 5
+LAG = 6
 MESH = pl.DeviceIdType.MESH
 NT = (((1,), (1,)), ((), ()))
 F32 = jnp.float32
@@ -63,8 +62,8 @@
     meta_s,
     row_acc,
     rows,
-    cols_a,
-    cols_b,
+    parts,
+    cols,
     cols_all,
     small_sem,
     raw_sem,
@@ -119,13 +118,6 @@
     def raw_copy(b):
         return pltpu.make_async_copy(root.at[b], raw.at[b], raw_sem.at[b])
 
-    barrier = pltpu.get_barrier_semaphore()
-    for k in range(1, SIDE):
-        pl.semaphore_signal(barrier, inc=1, device_id=along_y(k), device_id_type=MESH)
-        pl.semaphore_signal(barrier, inc=1, device_id=along_z(k), device_id_type=MESH)
-    for k in range(1, n_orig):
-        pl.semaphore_signal(barrier, inc=1, device_id=along_o(k), device_id_type=MESH)
-
     loads = [
         pltpu.make_async_copy(src, dst, small_sem.at[i])
         for i, (src, dst) in enumerate(
@@ -150,12 +142,21 @@
     lax.fori_loop(0, n_blocks, start_raw, 0)
     table_copy = pltpu.make_async_copy(prior, table, table_sem)
 
-    for load in loads:
-        load.wait()
+    barrier = pltpu.get_barrier_semaphore()
+    for k in range(1, SIDE):
+        pl.semaphore_signal(barrier, inc=1, device_id=along_y(k), device_id_type=MESH)
+        pl.semaphore_signal(barrier, inc=1, device_id=along_z(k), device_id_type=MESH)
+    for k in range(1, n_orig):
+        pl.semaphore_signal(barrier, inc=1, device_id=along_o(k), device_id_type=MESH)
+
+    loads[0].wait()
 
     target = lax.broadcasted_iota(I32, (S_T, S_T), 0)
     for c in range(n_root // S_T):
         concord_t[:, c * S_T : (c + 1) * S_T] = (target == sector_ref[c : c + 1, :]).astype(F32).astype(jnp.bfloat16)
+
+    for load in loads[1:]:
+        load.wait()
 
     lane = lax.broadcasted_iota(I32, (1, S_T), 1)
     to = lane % 16
@@ -211,20 +212,14 @@
                 pass_copy(h, way, b).start()
 
     lanes = lax.broadcasted_iota(I32, (S_T, S_T), 1)
-    row_acc[...] = jnp.zeros_like(row_acc)
-
-    def aggregate(b, carry):
+
+    def halves(b):
         raw_copy(b).wait()
-
-        @pl.when(b == LATE)
-        def _():
-            table_copy.start()
-
         left = jnp.dot(concord_t[...], raw[b], preferred_element_type=F32)
-        high, low = split(left)
-        both = lax.dot_general(
-            jnp.concatenate([high, low], axis=0), concord_t[...], NT, preferred_element_type=F32
-        )
+        return jnp.concatenate(split(left), axis=0)
+
+    def finish(b, stacked):
+        both = lax.dot_general(stacked, concord_t[...], NT, preferred_element_type=F32)
         block = (both[:S_T] + both[S_T:]) * present[0, b].astype(F32)
         a_0[b] = block[:HALF]
         b_0[b] = block[HALF:]
@@ -232,14 +227,22 @@
             gather_copy(0, k, b).start()
             gather_copy(1, k, b).start()
 
-        @pl.when(b >= LAG)
+    def aggregate(i, carry):
+        low = halves(2 * i)
+        high = halves(2 * i + 1)
+        finish(2 * i, low)
+        finish(2 * i + 1, high)
+
+        @pl.when(i == n_blocks // 2 - 2)
         def _():
-            forward(b - LAG)
-
-        sums = jnp.sum(block, axis=1, keepdims=True)
-        row_acc[...] += jnp.where(lanes == local_row[0, b], sums, 0.0)
-
-        @pl.when(b == 2)
+            table_copy.start()
+
+        @pl.when(i >= LAG // 2)
+        def _():
+            forward(2 * i - LAG)
+            forward(2 * i - LAG + 1)
+
+        @pl.when(i == 1)
         def _():
             for k in range(1, SIDE):
                 meta_y(k).wait()
@@ -248,7 +251,16 @@
 
         return carry
 
-    lax.fori_loop(0, n_blocks, aggregate, 0)
+    lax.fori_loop(0, n_blocks // 2, aggregate, 0)
+
+    upper = jnp.zeros((HALF, S_T), F32)
+    lower = jnp.zeros((HALF, S_T), F32)
+    for b in range(n_blocks):
+        here = lanes[:HALF] == local_row[0, b]
+        upper += jnp.where(here, jnp.sum(a_0[b], axis=1, keepdims=True), 0.0)
+        lower += jnp.where(here, jnp.sum(b_0[b], axis=1, keepdims=True), 0.0)
+    row_acc[:HALF] = upper
+    row_acc[HALF:] = lower
 
     table_copy.wait()
 
@@ -318,20 +330,6 @@
     fill(0, 1)
     send(0, 1)
     fill(1, 1)
-    send(1, 1)
-    fill(0, 3)
-    fill(1, 3)
-
-    def passed(b, carry):
-        for way in (0, 1):
-            pass_copy(0, way, b).wait_recv()
-            pass_copy(1, way, b).wait_recv()
-        return carry
-
-    lax.fori_loop(0, n_blocks, passed, 0)
-    fill(0, 2)
-    fill(1, 2)
-
     def wait_rows(i, carry):
         rows_copy(i).wait()
         return carry
@@ -345,60 +343,62 @@
     for r in range(tro):
         weights[r] = jnp.broadcast_to(upright[:, r : r + 1], (S_T, S_T))
 
-    col_of = lax.broadcasted_iota(I32, (trd, S_T), 0)
-
-    def line_cols(i, carry):
-        s = i % CAP
-        sums = list(carry)
-        for j in range(SIDE):
-            for h in (0, 1):
-                for k in range(SIDE):
-                    if h == 0:
-                        cell = meta_s[z, (y - j + SIDE) % SIDE, 0, y * SIDE + (z + k) % SIDE + 16 * (2 + s)]
-                        slot = pack_a[k, j, s]
-                    else:
-                        cell = meta_s[(z - j + SIDE) % SIDE, y, 0, ((y + k) % SIDE) * SIDE + z + 16 * (2 + s)]
-                        slot = pack_b[k, j, s]
-                    weight = weights[jnp.minimum(cell // trd, tro - 1), h * HALF : (h + 1) * HALF]
-                    line = jnp.sum(weight * slot, axis=0, keepdims=True)
-                    column = jnp.where(cell < tro * trd, cell % trd, trd)
-                    sums[h * SIDE + k] += jnp.where(col_of == column, line, 0.0)
-        return tuple(sums)
-
-    nothing = jnp.zeros((trd, S_T), F32)
-    sums = lax.fori_loop(0, CAP, line_cols, (nothing,) * (2 * SIDE))
-    for k in range(SIDE):
-        cols_a[k] = sums[k]
-        cols_b[k] = sums[SIDE + k]
-
-    def cols_copy(h, k):
-        held, along = (cols_a, along_z(k)) if h == 0 else (cols_b, along_y(k))
-        return remote(held.at[k], held.at[SIDE + k], cols_send.at[h, k - 1], cols_recv.at[h, k - 1], along)
-
-    for k in (2, 1, 3):
-        cols_copy(0, k).start()
-        cols_copy(1, k).start()
+    place = lax.broadcasted_iota(I32, parts.shape, 0) * trd + lax.broadcasted_iota(I32, parts.shape, 1)
+    spread = jnp.zeros(parts.shape, F32)
+    for b in range(n_blocks):
+        weight = weights[local_row[0, b]]
+        line = jnp.sum(weight[:HALF] * a_0[b] + weight[HALF:] * b_0[b], axis=0, keepdims=True)
+        here = place == owner[0, b] * trd + local_col[0, b]
+        spread += jnp.where(here, jnp.broadcast_to(line[None], parts.shape), 0.0)
+    parts[...] = spread
+    cols[d] = parts[d]
+
+    def cols_copy(i):
+        return remote(parts.at[(d + i) % n_dest], cols.at[d], cols_send.at[i - 1], cols_recv.at[i - 1], along_d(i))
+
+    def start_cols(i, carry):
+        cols_copy(i).start()
+        return carry
+
+    lax.fori_loop(1, n_dest, start_cols, 0)
+    send(1, 1)
+    fill(0, 3)
     send(0, 3)
+    fill(1, 3)
     send(1, 3)
-    send(0, 2)
-    send(1, 2)
 
     def prior_cols(r, carry):
         at = pl.multiple_of(r * S_T, S_T)
         weight = weights[r]
-        lines = [
-            jnp.sum(weight * table[pl.ds(at, S_T), c * S_T : (c + 1) * S_T], axis=0, keepdims=True)
-            for c in range(trd)
-        ]
+        lines = []
+        for c in range(trd):
+            columns = slice(c * S_T, (c + 1) * S_T)
+            scaled = weight * table[pl.ds(at, S_T), columns]
+            table[pl.ds(at, S_T), columns] = scaled
+            lines.append(jnp.sum(scaled, axis=0, keepdims=True))
         return carry + jnp.concatenate(lines, axis=0)
 
     wide = lax.fori_loop(0, tro, prior_cols, jnp.zeros((trd, S_T), F32))
 
-    wide += cols_a[0] + cols_b[0]
-    for k in range(1, SIDE):
-        cols_copy(0, k).wait()
-        cols_copy(1, k).wait()
-        wide += cols_a[SIDE + k] + cols_b[SIDE + k]
+    def passed(b, carry):
+        for way in (0, 1):
+            pass_copy(0, way, b).wait_recv()
+            pass_copy(1, way, b).wait_recv()
+        return carry
+
+    lax.fori_loop(0, n_blocks, passed, 0)
+    fill(0, 2)
+    send(0, 2)
+    fill(1, 2)
+    send(1, 2)
+
+    def wait_cols(i, carry):
+        cols_copy(i).wait()
+        return carry
+
+    lax.fori_loop(1, n_dest, wait_cols, 0)
+    for i in range(n_dest):
+        wide += cols[i]
     cols_all[o] = wide
 
     def cols_o(k):
@@ -406,6 +406,20 @@
 
     for k in range(1, n_orig):
         cols_o(k).start()
+
+    def sent(b, carry):
+        for h in (0, 1):
+            for way, k in ((0, 1), (1, 3)):
+                gather_copy(h, k, b).wait_send()
+                pass_copy(h, way, b).wait_send()
+        return carry
+
+    lax.fori_loop(0, n_blocks, sent, 0)
+    for j in (0, 1, 3, 2):
+        for k in (0, 1, 3, 2):
+            slot_copy(0, k, j).wait()
+            slot_copy(1, k, j).wait()
+
     for k in range(1, n_orig):
         cols_o(k).wait()
     total = cols_all[0]
@@ -413,28 +427,6 @@
         total += cols_all[i]
     col_factor[...] = col_target[...] / total
 
-    def scale(r, carry):
-        at = pl.multiple_of(r * S_T, S_T)
-        for c in range(trd):
-            columns = slice(c * S_T, (c + 1) * S_T)
-            table[pl.ds(at, S_T), columns] = weights[r] * table[pl.ds(at, S_T), columns] * col_factor[c : c + 1, :]
-        return carry
-
-    lax.fori_loop(0, tro, scale, 0)
-
-    def sent(b, carry):
-        for h in (0, 1):
-            for way, k in ((0, 1), (1, 3)):
-                gather_copy(h, k, b).wait_send()
-                pass_copy(h, way, b).wait_send()
-        return carry
-
-    lax.fori_loop(0, n_blocks, sent, 0)
-    for j in (0, 1, 3, 2):
-        for k in (0, 1, 3, 2):
-            slot_copy(0, k, j).wait()
-            slot_copy(1, k, j).wait()
-
 
 def place_kernel(meta, weights, col_factor, slots_a, slots_b, table_in, out, table, out_sem):
     trd = table.shape[1] // S_T
@@ -452,9 +444,8 @@
                 row = cell // trd
                 at = pl.multiple_of(row * S_T, S_T)
                 col = pl.multiple_of((cell % trd) * S_T, S_T)
-                across = col_factor[pl.ds(cell % trd, 1), :]
-                table[pl.ds(at, HALF), pl.ds(col, S_T)] += weights[row, :HALF] * slots_a[zs, ys, s] * across
-                table[pl.ds(at + HALF, HALF), pl.ds(col, S_T)] += weights[row, HALF:] * slots_b[ys, zs, s] * across
+                table[pl.ds(at, HALF), pl.ds(col, S_T)] += weights[row, :HALF] * slots_a[zs, ys, s]
+                table[pl.ds(at + HALF, HALF), pl.ds(col, S_T)] += weights[row, HALF:] * slots_b[ys, zs, s]
 
         return carry
 
@@ -465,6 +456,9 @@
         return pltpu.make_async_copy(table.at[pl.ds(at, S_T)], out.at[pl.ds(at, S_T)], out_sem.at[r])
 
     for r in range(tro):
+        for c in range(trd):
+            where = (slice(r * S_T, (r + 1) * S_T), slice(c * S_T, (c + 1) * S_T))
+            table[where] = table[where] * col_factor[c : c + 1, :]
         out_copy(r).start()
     for r in range(tro):
         out_copy(r).wait()
@@ -518,8 +512,8 @@
             pltpu.SMEM((SIDE, SIDE, 1, S_T), I32),
             pltpu.VMEM((S_T, S_T), F32),
             pltpu.VMEM((n_dest, tro, S_T), F32),
-            pltpu.VMEM((2 * SIDE, trd, S_T), F32),
-            pltpu.VMEM((2 * SIDE, trd, S_T), F32),
+            pltpu.VMEM((n_dest, trd, S_T), F32),
+            pltpu.VMEM((n_dest, trd, S_T), F32),
             pltpu.VMEM((n_orig, trd, S_T), F32),
             dma((7,)),
             dma((n_blocks,)),
@@ -536,8 +530,8 @@
             dma((2, SIDE - 1)),
             dma((n_dest - 1,)),
             dma((n_dest - 1,)),
-            dma((2, SIDE - 1)),
-            dma((2, SIDE - 1)),
+            dma((n_dest - 1,)),
+            dma((n_dest - 1,)),
             dma((n_orig - 1,)),
             dma((n_orig - 1,)),
         ],

time: 39.9 us -> 38.6 us (0.967)
  Pallas kernels: 39.8 us -> 38.5 us
    pallas_call x1, Pallas kernels: 37.1 us -> 35.7 us  [shards(): pl.pallas_call(route_kernel, out_shape=(got, got, jax.ShapeDtypeStruct((S...]
where the time goes in v3:
time: 38.6 us; the launch traced here: 38.5 us
  Pallas kernels  38.5 us (100%)
    pallas_call x1, Pallas kernels, shards(): pl.pallas_call(route_kernel, out_shape=(got, got, jax.ShapeDtypeStruct((S...  35.7 us
    pallas_call x1, Pallas kernels, shards(): pl.pallas_call(place_kernel, out_shape=(jax.ShapeDtypeStruct((rows_here,...  2.8 us

profile of v3, /device:TPU:1, one launch (start us, length us, event | category | flops | bytes accessed | tf_op | source)
XLA Modules:
  0.0 38.5 jit_solution(1668928368880942428)
XLA Ops:
  0.0 35.7 %route.1 = (f32[4,4,2,64,128]{4,3,2,1,0:T(8,128)S(1)}, f32[4,4,2,64,128]{4,3,2,1,0:T(8,128)S(1)}, s32[4,4,1,128]{3,2,1,0:T(1,128)S(1)}, f32[8,128,128]{2,1,0:T(8...) custom-call(s32[8,128]{1,0:T(8,128)} %bitcast.7, s32[1,8]{1,0:T(1,128)} %bitcast.10, s32[1,8]{1,0:T(1,128)} %bitcast.11, ...), custom_call_target="tpu_custom_call" | custom-call | tf_op jit(solution)/shard_map/route/pallas_call | solution.py:489
  35.7 2.8 %place.1 = (f32[1024,512]{1,0:T(8,128)}, f32[1024,512]{1,0:T(8,128)S(1)}) custom-call(s32[4,4,1,128]{3,2,1,0:T(1,128)S(1)} %get-tuple-element.12.meta, f32[8,128,128]{2,1,0:T(8,128)S(1)} %get-tuple-element.13.weights, f32[4,128]{1,0:T(4,128)S(1)} %get-tuple-element.14.col_factor, ...), custom_call_target="tpu_custom_call", output_to_operand_aliasing={{1}: (5, {})} | custom-call | tf_op jit(solution)/shard_map/place/pallas_call | solution.py:553

commit v4 on v3

--- a/solution.py
+++ b/solution.py
@@ -11,7 +11,7 @@
 HALF = S_T // 2
 CAP = 2
 SIDE = 4
-LAG = 6
+LAG = 4
 MESH = pl.DeviceIdType.MESH
 NT = (((1,), (1,)), ((), ()))
 F32 = jnp.float32
@@ -313,7 +313,7 @@
                     pack_b[k, j, s] = from_b[j][index]
 
     def send(h, j):
-        for k in (2, 1, 3, 0):
+        for k in (1, 3, 2, 0):
             slot_copy(h, k, j).start()
 
     fill(0, 0)
@@ -366,6 +366,18 @@
     send(0, 3)
     fill(1, 3)
     send(1, 3)
+
+    def passed(b, carry):
+        for way in (0, 1):
+            pass_copy(0, way, b).wait_recv()
+            pass_copy(1, way, b).wait_recv()
+        return carry
+
+    lax.fori_loop(0, n_blocks, passed, 0)
+    fill(0, 2)
+    send(0, 2)
+    fill(1, 2)
+    send(1, 2)
 
     def prior_cols(r, carry):
         at = pl.multiple_of(r * S_T, S_T)
@@ -379,18 +391,6 @@
         return carry + jnp.concatenate(lines, axis=0)
 
     wide = lax.fori_loop(0, tro, prior_cols, jnp.zeros((trd, S_T), F32))
-
-    def passed(b, carry):
-        for way in (0, 1):
-            pass_copy(0, way, b).wait_recv()
-            pass_copy(1, way, b).wait_recv()
-        return carry
-
-    lax.fori_loop(0, n_blocks, passed, 0)
-    fill(0, 2)
-    send(0, 2)
-    fill(1, 2)
-    send(1, 2)
 
     def wait_cols(i, carry):
         cols_copy(i).wait()

time: 38.6 us -> 37.9 us (0.982); the launches traced: 38.5 us -> 37.3 us
  Pallas kernels: 38.5 us -> 37.3 us
    pallas_call x1, Pallas kernels: 35.7 us -> 34.5 us  [shards(): pl.pallas_call(route_kernel, out_shape=(got, got, jax.ShapeDtypeStruct((S...]
where the time goes in v4:
time: 37.9 us; the launch traced here: 37.3 us
  Pallas kernels  37.3 us (98%)
    pallas_call x1, Pallas kernels, shards(): pl.pallas_call(route_kernel, out_shape=(got, got, jax.ShapeDtypeStruct((S...  34.5 us
    pallas_call x1, Pallas kernels, shards(): pl.pallas_call(place_kernel, out_shape=(jax.ShapeDtypeStruct((rows_here,...  2.78 us

profile of v4, /device:TPU:1, one launch (start us, length us, event | category | flops | bytes accessed | tf_op | source)
XLA Modules:
  0.0 37.3 jit_solution(3648161666906042039)
XLA Ops:
  0.0 34.5 %route.1 = (f32[4,4,2,64,128]{4,3,2,1,0:T(8,128)S(1)}, f32[4,4,2,64,128]{4,3,2,1,0:T(8,128)S(1)}, s32[4,4,1,128]{3,2,1,0:T(1,128)S(1)}, f32[8,128,128]{2,1,0:T(8...) custom-call(s32[8,128]{1,0:T(8,128)} %bitcast.7, s32[1,8]{1,0:T(1,128)} %bitcast.10, s32[1,8]{1,0:T(1,128)} %bitcast.11, ...), custom_call_target="tpu_custom_call" | custom-call | tf_op jit(solution)/shard_map/route/pallas_call | solution.py:489
  34.6 2.8 %place.1 = (f32[1024,512]{1,0:T(8,128)}, f32[1024,512]{1,0:T(8,128)S(1)}) custom-call(s32[4,4,1,128]{3,2,1,0:T(1,128)S(1)} %get-tuple-element.12.meta, f32[8,128,128]{2,1,0:T(8,128)S(1)} %get-tuple-element.13.weights, f32[4,128]{1,0:T(4,128)S(1)} %get-tuple-element.14.col_factor, ...), custom_call_target="tpu_custom_call", output_to_operand_aliasing={{1}: (5, {})} | custom-call | tf_op jit(solution)/shard_map/place/pallas_call | solution.py:553
